TPU v7x, 32 devices: a whole 2x2x4 slice. The times are simulated.
32 devices in a mesh: chain: 4 (over y, core), dp: 8 (over z, x).
Axes of the slice: x: 2, y: 2, z: 4, core: 2. Of those that a mesh axis runs over, the one named last changes fastest.
Arguments:
- train_features: float32 [256, 8, 8, 64], P('dp'), may hold values from -20 to 20
- train_labels: int32 [256], P('dp'), may hold values from 0 to 9
- test_features: float32 [512, 8, 8, 64], P('dp'), may hold values from -6 to 6
- conv_first: float32 [4, 9, 64, 64], P('chain'), may hold values from -0.25 to 0.25
- conv_second: float32 [4, 9, 64, 64], P('chain'), may hold values from -0.25 to 0.25
- norm_params: float32 [4, 6, 64], P('chain'), may hold values from -3 to 3
- head_weight: float32 [4, 64, 10], P('chain'), may hold values from -0.75 to 0.75
- head_bias: float32 [4, 10], P('chain'), may hold values from -3 to 3
- mom_first: float32 [4, 9, 64, 64], P('chain'), may hold values from -6 to 6
- mom_second: float32 [4, 9, 64, 64], P('chain'), may hold values from -6 to 6
- mom_norm: float32 [4, 6, 64], P('chain'), may hold values from -6 to 6
- mom_head: float32 [4, 64, 10], P('chain'), may hold values from -6 to 6
- mom_bias: float32 [4, 10], P('chain'), may hold values from -6 to 6
- step_size: float32 [4], P('chain'), may hold values from 0.001 to 0.003
Outputs:
- predictive: float32 [512, 10], P('dp')
- hamiltonians: float32 [4, 2], P('chain')
- potentials: float32 [4, 2], P('chain')
- forces: float32 [4, 2, 9, 64, 64], P('chain', None, None, 'dp')
All inputs are finite; a program needn't handle non-finite values.
Results may differ from a plain program's by a relative error of at most 0.0003.
Values sent between devices are 32-bit elements; how exact they have to be, the bound alone decides.
A program may use at most 128 MiB of HBM per device.

v0:
```python
import jax
import jax.numpy as jnp
from jax import lax
from jax.sharding import PartitionSpec as P

highest = lax.Precision.HIGHEST
epsilon = 1e-06


def conv_layer(inputs, kernel):
    height = inputs.shape[1]
    breadth = inputs.shape[2]
    padded = jnp.pad(inputs, ((0, 0), (1, 1), (1, 1), (0, 0)))
    total = jnp.zeros(inputs.shape[:3] + (kernel.shape[2],), jnp.float32)
    for offset in range(9):
        row_off = offset // 3
        col_off = offset % 3
        window = padded[:, row_off : row_off + height, col_off : col_off + breadth, :]
        total = total + jnp.einsum("bhwc,cd->bhwd", window, kernel[offset], precision=highest)
    return total


def normalize(values, gain, shift):
    moment = jnp.mean(values * values, axis=(1, 2), keepdims=True)
    return values * lax.rsqrt(moment + epsilon) * gain + shift


def network(params, features):
    kernel_one, kernel_two, norms, weights, biases = params
    hidden = jnp.maximum(normalize(conv_layer(features, kernel_one), norms[0], norms[1]), norms[2])
    branch = normalize(conv_layer(hidden, kernel_two), norms[3], norms[4])
    joined = jnp.maximum(features + branch, norms[5])
    pooled = jnp.mean(joined, axis=(1, 2))
    return jnp.dot(pooled, weights, precision=highest) + biases


def cross_sum(params, features, labels):
    logits = network(params, features)
    onehot = (labels[:, None] == jnp.arange(logits.shape[1], dtype=jnp.int32)[None, :]).astype(
        jnp.float32
    )
    return jnp.sum(jax.nn.logsumexp(logits, axis=1) - jnp.sum(onehot * logits, axis=1))


def squares_half(params):
    total = jnp.float32(0.0)
    for tensor in params:
        total = total + 0.5 * jnp.sum(tensor * tensor)
    return total


def own_columns(kernel):
    share_width = kernel.shape[1] // lax.axis_size("dp")
    return lax.dynamic_slice_in_dim(kernel, lax.axis_index("dp") * share_width, share_width, 1)


def kernel_forces(first_force, second_force):
    return jnp.stack([own_columns(first_force), own_columns(second_force)])[None]


def kinetic_total(shares):
    return squares_half(shares)


def reduce_all(cross, gradient, need_energy):
    kernels = ()
    others = tuple(gradient)
    summed = lax.psum(others, "dp")
    total = cross
    if need_energy:
        total = lax.psum(cross, "dp")
    return (total, kernels + tuple(summed))


def shards(
    train_features,
    train_labels,
    test_features,
    conv_first,
    conv_second,
    norm_params,
    head_weight,
    head_bias,
    mom_first,
    mom_second,
    mom_norm,
    mom_head,
    mom_bias,
    step_size,
):
    start_pos = (conv_first[0], conv_second[0], norm_params[0], head_weight[0], head_bias[0])
    start_mom = (mom_first[0], mom_second[0], mom_norm[0], mom_head[0], mom_bias[0])
    stride = step_size[0]
    value_grad = jax.value_and_grad(cross_sum)

    def evaluate(whole, shares, need_energy):
        cross, gradient = value_grad(whole, train_features, train_labels)
        total, summed = reduce_all(cross, gradient, need_energy)
        summed = tuple((grad_val + pos_val for grad_val, pos_val in zip(summed, shares)))
        return (total + squares_half(whole), summed)

    whole = start_pos
    shares = start_pos
    momentum = start_mom
    energy_start, grad_start = evaluate(whole, shares, True)
    momentum = tuple(
        (mom_val - 0.5 * stride * grad_val for mom_val, grad_val in zip(momentum, grad_start))
    )
    shares = tuple((pos_val + stride * mom_val for pos_val, mom_val in zip(shares, momentum)))
    whole = shares
    unused, grad_middle = evaluate(whole, shares, False)
    momentum = tuple(
        (mom_val - stride * grad_val for mom_val, grad_val in zip(momentum, grad_middle))
    )
    shares = tuple((pos_val + stride * mom_val for pos_val, mom_val in zip(shares, momentum)))
    whole = shares
    energy_end, grad_end = evaluate(whole, shares, True)
    momentum = tuple(
        (mom_val - 0.5 * stride * grad_val for mom_val, grad_val in zip(momentum, grad_end))
    )
    pair = jnp.stack([energy_start + squares_half(start_mom), energy_end + kinetic_total(momentum)])
    pot_pair = jnp.stack([energy_start, energy_end])
    first_force = 0.5 * grad_start[0] + grad_middle[0] + 0.5 * grad_end[0]
    second_force = 0.5 * grad_start[1] + grad_middle[1] + 0.5 * grad_end[1]
    forces = kernel_forces(first_force, second_force)
    probs = jax.nn.softmax(network(whole, test_features), axis=-1)
    predictive = lax.psum(probs, "chain") / lax.axis_size("chain")
    return (predictive, jnp.reshape(pair, (1, 2)), jnp.reshape(pot_pair, (1, 2)), forces)


def solution(mesh):
    placed = (
        P("dp", None, None, None),
        P("dp"),
        P("dp", None, None, None),
        P("chain", None, None, None),
        P("chain", None, None, None),
        P("chain", None, None),
        P("chain", None, None),
        P("chain", None),
        P("chain", None, None, None),
        P("chain", None, None, None),
        P("chain", None, None),
        P("chain", None, None),
        P("chain", None),
        P("chain"),
    )
    return jax.shard_map(
        shards,
        mesh=mesh,
        in_specs=placed,
        out_specs=(
            P("dp", None),
            P("chain", None),
            P("chain", None),
            P("chain", None, None, "dp", None),
        ),
        check_vma=False,
    )
```

profile of v0, /device:TPU:0, one launch (start us, length us, event | category | flops | bytes accessed | tf_op | source)
XLA Modules:
  0.0 629.0 jit_solution(16154514784072550631)
XLA Ops:
  7.2 2.9 fusion.52
  70.3 2.5 convolution_bitcast_fusion.55
  82.8 39.1 %all-reduce.107 = (f32[64,10]{0,1:T(8,128)S(1)}, f32[6,64]{1,0:T(8,128)S(1)}, f32[10]{0:T(128)S(1)}) all-reduce(f32[64,10]{0,1:T(8,128)S(1)} %fusion.148, f32[6,64]{1,0:T(8,128)S(1)} %pad_add_fusion.23, f32[10]{0:T(128)S(1)} %get-tuple-element.33), channel_id=1, replica_groups=mesh['chain'=4,'dp'=8] {'dp'}, use_global_device_ids=true, to_apply=%region_19.20 | all-reduce | flops 1034 | bytes 8272 | tf_op jit(solution)/shard_map/psum | solution.py:68
  123.8 34.0 %all-reduce.119.cloned.1.call-done = (f32[9,64,64]{2,1,0:T(8,128)}, f32[9,64,64]{2,1,0:T(8,128)}) async-done(((f32[9,64,64]{2,1,0:T(8,128)}, f32[9,64,64]{2,1,0:T(8,128)}), (f32[9,64,64]{2,1,0:T(8,128)}, f32[9,64,64]{2,1,0:T(8,128)})) %all-reduce.119.cloned.1.call-update) | async-done | bytes 294928 | tf_op jit(solution)/shard_map/psum | solution.py:68
  222.1 2.5 convolution_bitcast_fusion.53
  232.1 35.2 %all-reduce.106 = (f32[64,10]{0,1:T(8,128)S(1)}, f32[6,64]{1,0:T(8,128)S(1)}, f32[10]{0:T(128)S(1)}) all-reduce(f32[64,10]{0,1:T(8,128)S(1)} %fusion.145, f32[6,64]{1,0:T(8,128)S(1)} %pad_add_fusion.22, f32[10]{0:T(128)S(1)} %fusion.179), channel_id=1, replica_groups=mesh['chain'=4,'dp'=8] {'dp'}, use_global_device_ids=true, to_apply=%region_38.39 | all-reduce | flops 1034 | bytes 8272 | tf_op jit(solution)/shard_map/psum | solution.py:68
  270.4 68.7 %all-reduce.117.cloned.1.call-done = (f32[9,64,64]{2,1,0:T(8,128)}, f32[9,64,64]{2,1,0:T(8,128)}) async-done(((f32[9,64,64]{2,1,0:T(8,128)}, f32[9,64,64]{2,1,0:T(8,128)}), (f32[9,64,64]{2,1,0:T(8,128)}, f32[9,64,64]{2,1,0:T(8,128)})) %all-reduce.117.cloned.1.call-update) | async-done | bytes 294928 | tf_op jit(solution)/shard_map/psum | solution.py:68
  403.1 2.7 convolution_bitcast_fusion.10
  405.8 2.8 convolution_bitcast_fusion.11
  408.6 2.5 convolution_bitcast_fusion.12
  411.1 3.0 convolution_bitcast_fusion.13
  414.1 3.1 convolution_bitcast_fusion.51
  417.2 2.8 convolution_bitcast_fusion.14
  431.6 3.1 fusion.20
  434.7 3.3 fusion.30
  438.0 3.3 fusion.22
  441.2 3.5 fusion.24
  444.7 3.2 fusion.26
  447.9 2.9 fusion.28
  450.9 2.9 multiply_reduce_fusion.1
  453.8 3.5 fusion.134
  457.3 3.2 fusion.125
  460.4 3.2 fusion.127
  463.6 3.1 fusion.129
  466.7 3.2 fusion.131
  470.0 3.2 fusion.136
  473.2 3.1 fusion.138
  476.4 3.5 fusion.139
  482.0 35.7 %all-reduce.105 = (f32[]{:T(128)}, f32[6,64]{1,0:T(8,128)S(1)}, f32[64,10]{0,1:T(8,128)S(1)}, f32[10]{0:T(128)S(1)}, f32[]{:T(128)}) all-reduce(f32[]{:T(128)} %subtract_reduce_fusion, f32[6,64]{1,0:T(8,128)S(1)} %pad_add_fusion.21, f32[64,10]{0,1:T(8,128)S(1)} %copy-done.41, ...), channel_id=1, replica_groups=mesh['chain'=4,'dp'=8] {'dp'}, use_global_device_ids=true, to_apply=%region_64.65 | all-reduce | flops 1036 | bytes 8288 | tf_op jit(solution)/shard_map/psum | solution.py:71
  523.8 7.9 %multiply_reduce_fusion = (f32[64,64]{1,0:T(8,128)S(1)}, f32[64,8,8,64]{3,0,2,1:T(8,128)S(1)}) fusion(f32[9,64,64]{2,1,0:T(8,128)S(1)} %get-tuple-element.66, f32[64,8,8,64]{3,0,2,1:T(8,128)S(1)} %get-tuple-element.129, f32[64]{0:T(128)S(1)} %get-tuple-element.99, f32[64]{0:T(128)S(1)} %get-tuple-element.100, f32[64]{0:T(128)S(1)} %get-tuple-element.101, ...), kind=kOutput, calls=%fused_computation.6 | convolution fusion | flops 157806592 | bytes 11617792 | tf_op jit(solution)/shard_map/bhwc,cd->bhwd/dot_general | solution.py:19
  533.5 5.8 psum.136
  543.4 69.4 %all-reduce.115.cloned.1.call-done = (f32[9,64,64]{2,1,0:T(8,128)}, f32[9,64,64]{2,1,0:T(8,128)}) async-done(((f32[9,64,64]{2,1,0:T(8,128)}, f32[9,64,64]{2,1,0:T(8,128)}), (f32[9,64,64]{2,1,0:T(8,128)}, f32[9,64,64]{2,1,0:T(8,128)})) %all-reduce.115.cloned.1.call-update) | async-done | bytes 294928 | tf_op jit(solution)/shard_map/psum | solution.py:68
  (365 shorter events, 229.6 us)
Async XLA Ops:
  7.2 150.6 %all-reduce.119.cloned.1.call-start = ((), (), s32[]{:S(2)}) async-start(), calls=%async_computation.2 | async-start | bytes 1179648 | tf_op jit(solution)/shard_map/psum | solution.py:68
  78.6 43.3 %copy-start.71 = (f32[1,10]{1,0:T(1,128)S(1)}, f32[1,10]{1,0:T(1,128)}, u32[]{:S(2)}) copy-start(f32[1,10]{1,0:T(1,128)} %param.26) | copy-start | bytes 124
  78.7 43.8 %copy-start.58 = (f32[1,6,64]{2,0,1:T(1,128)S(1)}, f32[1,6,64]{2,0,1:T(1,128)}, u32[]{:S(2)}) copy-start(f32[1,6,64]{2,0,1:T(1,128)} %param.24) | copy-start | bytes 4612
  78.7 79.1 %copy-start.12 = (f32[1,9,64,64]{3,2,1,0:T(8,128)S(1)}, f32[1,9,64,64]{3,2,1,0:T(8,128)}, u32[]{:S(2)}) copy-start(f32[1,9,64,64]{3,2,1,0:T(8,128)} %param.22) | copy-start | bytes 442372
  81.8 257.3 %all-reduce.117.cloned.1.call-start = ((), (), s32[]{:S(2)}) async-start(), calls=%async_computation.1 | async-start | bytes 1179648 | tf_op jit(solution)/shard_map/psum | solution.py:68
  122.5 146.6 %copy-start.56 = (f32[10]{0:T(128)}, f32[10]{0:T(128)S(1)}, u32[]{:S(2)}) copy-start(f32[10]{0:T(128)S(1)} %get-tuple-element.80) | copy-start | bytes 124
  123.2 144.1 %copy-start.39 = (f32[6,64]{1,0:T(8,128)}, f32[6,64]{1,0:T(8,128)S(1)}, u32[]{:S(2)}) copy-start(f32[6,64]{1,0:T(8,128)S(1)} %get-tuple-element.84) | copy-start | bytes 4612
  159.4 179.7 %copy-start.5 = (f32[9,64,64]{2,1,0:T(8,128)}, f32[9,64,64]{2,1,0:T(8,128)S(1)}, u32[]{:S(2)}) copy-start(f32[9,64,64]{2,1,0:T(8,128)S(1)} %get-tuple-element.86) | copy-start | bytes 442372
  173.1 181.5 %copy-start.7 = (f32[9,64,64]{2,1,0:T(8,128)}, f32[9,64,64]{2,1,0:T(8,128)S(1)}, u32[]{:S(2)}) copy-start(f32[9,64,64]{2,1,0:T(8,128)S(1)} %get-tuple-element.88) | copy-start | bytes 442372
  267.2 75.9 %copy-start.42 = (f32[64,10]{0,1:T(8,128)}, f32[64,10]{0,1:T(8,128)S(1)}, u32[]{:S(2)}) copy-start(f32[64,10]{0,1:T(8,128)S(1)} %get-tuple-element.51) | copy-start | bytes 7684
  267.2 75.9 %copy-start.46 = (f32[6,64]{1,0:T(8,128)}, f32[6,64]{1,0:T(8,128)S(1)}, u32[]{:S(2)}) copy-start(f32[6,64]{1,0:T(8,128)S(1)} %get-tuple-element.52) | copy-start | bytes 4612
  267.2 75.9 %copy-start.68 = (f32[10]{0:T(128)}, f32[10]{0:T(128)S(1)}, u32[]{:S(2)}) copy-start(f32[10]{0:T(128)S(1)} %get-tuple-element.53) | copy-start | bytes 124
  267.3 97.9 %copy-start.52 = (f32[64]{0:T(128)}, f32[64]{0:T(128)S(1)}, u32[]{:S(2)}) copy-start(f32[64]{0:T(128)S(1)} %get-tuple-element.98) | copy-start | bytes 772
  267.3 100.5 %copy-start.50 = (f32[64]{0:T(128)}, f32[64]{0:T(128)S(1)}, u32[]{:S(2)}) copy-start(f32[64]{0:T(128)S(1)} %get-tuple-element.97) | copy-start | bytes 772
  267.3 102.2 %copy-start.48 = (f32[64]{0:T(128)}, f32[64]{0:T(128)S(1)}, u32[]{:S(2)}) copy-start(f32[64]{0:T(128)S(1)} %get-tuple-element.96) | copy-start | bytes 772
  268.8 344.0 %all-reduce.115.cloned.1.call-start = ((), (), s32[]{:S(2)}) async-start(), calls=%async_computation | async-start | bytes 1179648 | tf_op jit(solution)/shard_map/psum | solution.py:68
  269.1 96.8 %copy-start.65 = (f32[10]{0:T(128)}, f32[10]{0:T(128)S(1)}, u32[]{:S(2)}) copy-start(f32[10]{0:T(128)S(1)} %multiply_add_fusion.13) | copy-start | bytes 124
  341.5 109.4 %copy-start.3 = (f32[9,64,64]{2,1,0:T(8,128)}, f32[9,64,64]{2,1,0:T(8,128)S(1)}, u32[]{:S(2)}) copy-start(f32[9,64,64]{2,1,0:T(8,128)S(1)} %get-tuple-element.69) | copy-start | bytes 442372
  476.4 42.0 %copy-start.40 = (f32[6,64]{1,0:T(8,128)S(1)}, f32[6,64]{1,0:T(8,128)}, u32[]{:S(2)}) copy-start(f32[6,64]{1,0:T(8,128)} %copy-done.39) | copy-start | bytes 4612
  476.4 42.0 %copy-start.45 = (f32[6,64]{1,0:T(8,128)S(1)}, f32[6,64]{1,0:T(8,128)}, u32[]{:S(2)}) copy-start(f32[6,64]{1,0:T(8,128)} %copy-done.44) | copy-start | bytes 4612
  476.4 42.0 %copy-start.47 = (f32[6,64]{1,0:T(8,128)S(1)}, f32[6,64]{1,0:T(8,128)}, u32[]{:S(2)}) copy-start(f32[6,64]{1,0:T(8,128)} %copy-done.46) | copy-start | bytes 4612
  476.4 44.1 %copy-start.55 = (f32[1,10]{1,0:T(1,128)S(1)}, f32[1,10]{1,0:T(1,128)}, u32[]{:S(2)}) copy-start(f32[1,10]{1,0:T(1,128)} %param.21) | copy-start | bytes 124
  476.4 44.1 %copy-start.57 = (f32[10]{0:T(128)S(1)}, f32[10]{0:T(128)}, u32[]{:S(2)}) copy-start(f32[10]{0:T(128)} %copy-done.56) | copy-start | bytes 124
  476.4 44.1 %copy-start.66 = (f32[10]{0:T(128)S(1)}, f32[10]{0:T(128)}, u32[]{:S(2)}) copy-start(f32[10]{0:T(128)} %copy-done.65) | copy-start | bytes 124
  476.4 44.1 %copy-start.69 = (f32[10]{0:T(128)S(1)}, f32[10]{0:T(128)}, u32[]{:S(2)}) copy-start(f32[10]{0:T(128)} %copy-done.68) | copy-start | bytes 124
  531.9 80.9 %copy-start.4 = (f32[9,64,64]{2,1,0:T(8,128)S(1)}, f32[9,64,64]{2,1,0:T(8,128)}, u32[]{:S(2)}) copy-start(f32[9,64,64]{2,1,0:T(8,128)} %copy-done.3) | copy-start | bytes 442372
  531.9 80.9 %copy-start.6 = (f32[9,64,64]{2,1,0:T(8,128)S(1)}, f32[9,64,64]{2,1,0:T(8,128)}, u32[]{:S(2)}) copy-start(f32[9,64,64]{2,1,0:T(8,128)} %copy-done.5) | copy-start | bytes 442372
  531.9 80.9 %copy-start.8 = (f32[9,64,64]{2,1,0:T(8,128)S(1)}, f32[9,64,64]{2,1,0:T(8,128)}, u32[]{:S(2)}) copy-start(f32[9,64,64]{2,1,0:T(8,128)} %copy-done.7) | copy-start | bytes 442372
  531.9 80.9 %copy-start.11 = (f32[1,9,64,64]{3,2,1,0:T(8,128)S(1)}, f32[1,9,64,64]{3,2,1,0:T(8,128)}, u32[]{:S(2)}) copy-start(f32[1,9,64,64]{3,2,1,0:T(8,128)} %param.23) | copy-start | bytes 442372
  532.0 80.9 %copy-start.13 = (f32[1,9,64,64]{3,2,1,0:T(8,128)S(1)}, f32[1,9,64,64]{3,2,1,0:T(8,128)}, u32[]{:S(2)}) copy-start(f32[1,9,64,64]{3,2,1,0:T(8,128)} %param.22) | copy-start | bytes 442372
  532.0 80.9 %copy-start.14 = (f32[9,64,64]{2,1,0:T(8,128)S(1)}, f32[9,64,64]{2,1,0:T(8,128)}, u32[]{:S(2)}) copy-start(f32[9,64,64]{2,1,0:T(8,128)} %get-tuple-element.70) | copy-start | bytes 442372
  532.0 80.9 %copy-start.15 = (f32[9,64,64]{2,1,0:T(8,128)S(1)}, f32[9,64,64]{2,1,0:T(8,128)}, u32[]{:S(2)}) copy-start(f32[9,64,64]{2,1,0:T(8,128)} %get-tuple-element.67) | copy-start | bytes 442372
  (43 other events, 295.0 us)
Sparse Core Ops, SparseCore 0:
  81.9 75.8 all-reduce.118
  268.9 70.1 all-reduce.116
  542.3 70.4 all-reduce.114
where the time goes:
time: 638 us; the launch traced here: 629 us
  matrix products  275 us (43%)
  waiting for transfers between devices  172 us (27%)
  blocking collectives  116 us (18%)
  other arithmetic  35 us (5%)
  between operations  30.8 us (5%)
    dot_general x141, matrix products, conv_layer(): jnp.einsum('bhwc,cd->bhwd', window, kernel[offset], precision=highest)  253 us
    psum x3, waiting for transfers between devices, reduce_all(): summed = lax.psum(others, 'dp')  172 us
    psum x2, blocking collectives, reduce_all(): summed = lax.psum(others, 'dp')  74.3 us
    psum x1, blocking collectives, reduce_all(): total = lax.psum(cross, 'dp')  35.7 us
    pad x12, matrix products, conv_layer(): window = padded[:, row_off:row_off + height, col_off:col_off + breadth, :]  18.8 us
  transfers between devices with their start and end apart: 3, of which 3 were waited for; matrix products, arithmetic and copies ran while one was open for 1% of the time, Pallas kernels for 0%

commit v1 on v0

v1 whole, which is shorter than its diff:
```python
import functools

import jax
import jax.numpy as jnp
from jax import lax
from jax.experimental import pallas as pl
from jax.experimental.pallas import tpu as pltpu
from jax.sharding import PartitionSpec as P

MESH = pl.DeviceIdType.MESH
HIGHEST = lax.Precision.HIGHEST
EPS = 1e-6
CH = 64
TAPS = 9
SMALL = 24
F32 = jnp.float32
BF16 = jnp.bfloat16


def split(value):
    high = value.astype(BF16)
    return high, (value - high.astype(F32)).astype(BF16)


def mm(left, right):
    return jnp.dot(left, right, preferred_element_type=F32)


def put_weights(ref, taps):
    zero = jnp.zeros((CH, CH), F32)
    for a in range(3):
        mine = taps[3 * a : 3 * a + 3]
        left = jnp.concatenate(mine + [zero], axis=0)
        right = jnp.concatenate([zero] + mine, axis=0)
        high, low = split(jnp.concatenate([left, right], axis=1))
        ref[256 * a : 256 * a + 256, 0:128] = high
        ref[256 * a : 256 * a + 256, 128:256] = low


def put_padded(hs, ls, value, images):
    rows, width = value.shape
    edge = jnp.zeros((rows, CH), F32)
    high, low = split(jnp.concatenate([edge, value, edge], axis=1))
    block = jnp.zeros((images, width + 2 * CH), BF16)
    for ref, val in ((hs, high), (ls, low)):
        ref[0:images, :] = block
        ref[images : images + rows, :] = val
        ref[images + rows : 2 * images + rows, :] = block


def conv(hs, ls, weights, images):
    rows = hs.shape[0] - 2 * images
    outs = []
    for p in range((hs.shape[1] - 128) // 128):
        def window(ref):
            return jnp.concatenate(
                [ref[a * images : a * images + rows, 128 * p : 128 * p + 256] for a in range(3)], axis=1
            )
        both = mm(window(hs), weights[...])
        outs.append(both[:, :128] + both[:, 128:] + mm(window(ls), weights[:, :128]))
    return jnp.concatenate(outs, axis=1)


def kernel_grad(value, hs, ls, images):
    rows, width = value.shape
    high, low = split(value.T)
    totals = [None] * 3
    for p in range(width // 128):
        part_high = high[128 * p : 128 * p + 128]
        stacked = jnp.concatenate([part_high, low[128 * p : 128 * p + 128]], axis=0)
        for a in range(3):
            start = (2 - a) * images
            both = mm(stacked, hs[start : start + rows, 128 * p : 128 * p + 256])
            both = both[:128] + both[128:]
            both = both + mm(part_high, ls[start : start + rows, 128 * p : 128 * p + 256])
            totals[a] = both if totals[a] is None else totals[a] + both
    grads = []
    for a in range(3):
        for b in range(3):
            grads.append(
                totals[a][0:64, (2 - b) * 64 : (3 - b) * 64] + totals[a][64:128, (3 - b) * 64 : (4 - b) * 64]
            )
    return grads


def over_columns(value):
    width = value.shape[1]
    shift = width // 2
    while shift >= CH:
        value = value + pltpu.roll(value, shift, 1)
        shift //= 2
    return value


def over_pixels(value, images):
    total = value[0:images]
    for h in range(1, value.shape[0] // images):
        total = total + value[h * images : (h + 1) * images]
    return over_columns(total)


def spread(value, rows):
    return jnp.concatenate([value] * (rows // value.shape[0]), axis=0)


def wide(row, width):
    return jnp.concatenate([row] * (width // CH), axis=1)


def above(value, bound):
    return jnp.where(value > bound, 1.0, jnp.where(value == bound, 0.5, 0.0))


def load_taps(theta, columns):
    shards = theta.shape[0]
    per = CH // shards
    return [
        jnp.concatenate([theta[s, t * per : (t + 1) * per, columns] for s in range(shards)], axis=0)
        for t in range(TAPS)
    ]


def forward(x, theta, small, images, refs):
    hs, ls, ys, yl, w_one, w_two = refs
    rows, width = x.shape
    pixels = rows // images * (width // CH)
    taps_two = load_taps(theta, slice(64, 128))
    put_weights(w_one, load_taps(theta, slice(0, 64)))
    put_weights(w_two, taps_two)
    norms = [wide(small[k : k + 1, 0:64], width) for k in range(6)]
    put_padded(hs, ls, x, images)
    c1 = conv(hs, ls, w_one, images)
    r1 = spread(lax.rsqrt(over_pixels(c1 * c1, images) / pixels + EPS), rows)
    u1 = c1 * r1
    v1 = u1 * norms[0] + norms[1]
    y = jnp.maximum(v1, norms[2])
    put_padded(ys, yl, y, images)
    c2 = conv(ys, yl, w_two, images)
    r2 = spread(lax.rsqrt(over_pixels(c2 * c2, images) / pixels + EPS), rows)
    u2 = c2 * r2
    t = x + (u2 * norms[3] + norms[4])
    pooled = (over_pixels(jnp.maximum(t, norms[5]), images) / pixels)[:, 0:64]
    head = small[8:24, 0:64]
    logits = lax.dot_general(
        pooled, head, (((1,), (1,)), ((), ())), precision=HIGHEST, preferred_element_type=F32
    ) + small[6:7, 0:16]
    return norms, taps_two, r1, u1, v1, y, r2, u2, t, pooled, head, logits


def soft(logits, classes):
    valid = lax.broadcasted_iota(jnp.int32, logits.shape, 1) < classes
    top = jnp.max(jnp.where(valid, logits, -jnp.inf), axis=1, keepdims=True)
    powers = jnp.where(valid, jnp.exp(jnp.where(valid, logits - top, 0.0)), 0.0)
    total = jnp.sum(powers, axis=1, keepdims=True)
    return powers / total, top + jnp.log(total)


def grad_kernel(classes, x_ref, hot_ref, theta, small, out, hs, ls, ys, yl, w_one, w_two, w_back):
    x = x_ref[...]
    rows, width = x.shape
    images = hot_ref.shape[0]
    pixels = rows // images * (width // CH)
    norms, taps_two, r1, u1, v1, y, r2, u2, t, pooled, head, logits = forward(
        x, theta, small, images, (hs, ls, ys, yl, w_one, w_two)
    )
    hot = hot_ref[...]
    probs, lse = soft(logits, classes)
    cross = jnp.sum(lse - jnp.sum(hot * logits, axis=1, keepdims=True), axis=0, keepdims=True)
    dlog = probs - hot
    dhead = lax.dot_general(dlog, pooled, (((0,), (0,)), ((), ())), precision=HIGHEST, preferred_element_type=F32)
    dbias = jnp.sum(dlog, axis=0, keepdims=True)
    dpool = jnp.dot(dlog, head, precision=HIGHEST, preferred_element_type=F32) / pixels
    dout = spread(wide(dpool, width), rows)
    keep = above(t, norms[5])
    dz = dout * keep

    def by_channel(value):
        return over_columns(jnp.sum(value, axis=0, keepdims=True))[:, 0:64]

    dn5 = by_channel(dout - dz)
    dn4 = by_channel(dz)
    dn3 = by_channel(dz * u2)
    du = dz * norms[3]
    g2 = r2 * (du - u2 * spread(over_pixels(du * u2, images) / pixels, rows))
    put_weights(w_back, [tap.T for tap in reversed(taps_two)])
    put_padded(hs, ls, g2, images)
    grads_two = kernel_grad(y, hs, ls, images)
    dy = conv(hs, ls, w_back, images)
    dv = dy * above(v1, norms[2])
    dn2 = by_channel(dy - dv)
    dn1 = by_channel(dv)
    dn0 = by_channel(dv * u1)
    du = dv * norms[0]
    g1 = r1 * (du - u1 * spread(over_pixels(du * u1, images) / pixels, rows))
    put_padded(ys, yl, g1, images)
    grads_one = kernel_grad(x, ys, yl, images)
    shards = out.shape[0]
    per = CH // shards
    base = TAPS * per
    tail = jnp.zeros((1, 112), F32)
    half = jnp.zeros((1, 64), F32)
    block = jnp.concatenate(
        [jnp.concatenate([row, half], axis=1) for row in (dn0, dn1, dn2, dn3, dn4, dn5)]
        + [jnp.concatenate([dbias, tail], axis=1), jnp.broadcast_to(cross, (1, 128))]
        + [jnp.concatenate([dhead, jnp.zeros((16, 64), F32)], axis=1)],
        axis=0,
    )
    for tap in range(TAPS):
        both = jnp.concatenate([grads_one[tap], grads_two[tap]], axis=1)
        for s in range(shards):
            out[s, tap * per : (tap + 1) * per, :] = both[s * per : (s + 1) * per]
    for s in range(shards):
        out[s, base : base + SMALL, :] = block


def test_kernel(classes, x_ref, theta, small, out, hs, ls, ys, yl, w_one, w_two):
    images = out.shape[0]
    logits = forward(x_ref[...], theta, small, images, (hs, ls, ys, yl, w_one, w_two))[-1]
    out[...] = jnp.concatenate([soft(logits, classes)[0], jnp.zeros((images, 112), F32)], axis=1)


def compute_scratch(rows, width, images, backward):
    padded = pltpu.VMEM((rows + 2 * images, width + 128), BF16)
    return [padded] * 4 + [pltpu.VMEM((768, 256), BF16)] * (3 if backward else 2)


def vmem():
    return pl.BlockSpec(memory_space=pltpu.VMEM)


def greet(axes):
    barrier = pltpu.get_barrier_semaphore()
    count = 0
    for axis in axes:
        n = lax.axis_size(axis)
        me = lax.axis_index(axis)
        for k in range(1, n):
            pl.semaphore_signal(barrier, inc=1, device_id={axis: lax.rem(me + k, n)}, device_id_type=MESH)
        count += n - 1
    pl.semaphore_wait(barrier, count)


def send_all(axis, source, slot, send_sem, recv_sem):
    n = lax.axis_size(axis)
    me = lax.axis_index(axis)
    copies = []
    for k in range(1, n):
        peer = lax.rem(me + k, n)
        copy = pltpu.make_async_remote_copy(
            src_ref=source(peer), dst_ref=slot(me), send_sem=send_sem.at[k], recv_sem=recv_sem.at[k],
            device_id={axis: peer}, device_id_type=MESH,
        )
        copy.start()
        copies.append(copy)
    return copies


def finish(copies):
    for copy in copies:
        copy.wait_recv()
    for copy in copies:
        copy.wait_send()


def in_order(ref):
    total = ref[0]
    for s in range(1, ref.shape[0]):
        total = total + ref[s]
    return total


def move_kernel(factor, step, grads, theta, mom, small, small_mom,
                theta_all, new_mom, new_small, new_small_mom, force, sums, got, mine, send_a, recv_a, send_b, recv_b):
    me = lax.axis_index("dp")
    base = mom.shape[0]
    h = step[0]
    greet(("dp",))
    copies = send_all("dp", lambda s: grads.at[s], lambda s: got.at[s], send_a, recv_a)
    got[me] = grads[me]
    finish(copies)
    total = in_order(got)
    grad = total[0:base] + theta[me]
    mom_next = mom[...] - (factor * h) * grad
    mine[...] = theta[me] + h * mom_next
    copies = send_all("dp", lambda s: mine, lambda s: theta_all.at[s], send_b, recv_b)
    theta_all[me] = mine[...]
    new_mom[...] = mom_next
    force[...] = grad
    sums[...] = total[base : base + SMALL]
    real = lax.broadcasted_iota(jnp.int32, (SMALL, 128), 0) != 7
    small_grad = jnp.where(real, total[base : base + SMALL] + small[...], 0.0)
    small_next = small_mom[...] - (factor * h) * small_grad
    new_small_mom[...] = small_next
    new_small[...] = small[...] + h * small_next
    finish(copies)


def last_kernel(step, grads, theta, mom, small, small_mom, force_a, force_b, probs,
                force, sums, kinetic, mean, got, mine, parts, seen, send_a, recv_a, send_b, recv_b, send_c, recv_c):
    me = lax.axis_index("dp")
    chain = lax.axis_index("chain")
    base = mom.shape[0]
    h = step[0]
    greet(("dp", "chain"))
    copies = send_all("dp", lambda s: grads.at[s], lambda s: got.at[s], send_a, recv_a)
    others = send_all("chain", lambda s: probs, lambda s: seen.at[s], send_c, recv_c)
    got[me] = grads[me]
    seen[chain] = probs[...]
    finish(copies)
    total = in_order(got)
    grad = total[0:base] + theta[me]
    mom_next = mom[...] - (0.5 * h) * grad
    mine[...] = jnp.broadcast_to(jnp.sum(mom_next * mom_next, axis=0, keepdims=True), (8, 128))
    copies = send_all("dp", lambda s: mine, lambda s: parts.at[s], send_b, recv_b)
    parts[me] = mine[...]
    force[...] = 0.5 * force_a[...] + force_b[...] + 0.5 * grad
    sums[...] = total[base : base + SMALL]
    real = lax.broadcasted_iota(jnp.int32, (SMALL, 128), 0) != 7
    small_grad = jnp.where(real, total[base : base + SMALL] + small[...], 0.0)
    small_next = small_mom[...] - (0.5 * h) * small_grad
    finish(others)
    mean[...] = in_order(seen) / lax.axis_size("chain")
    finish(copies)
    kinetic[...] = in_order(parts)[0:1] + jnp.sum(small_next * small_next, axis=0, keepdims=True)


def pack_small(norms, head, bias):
    classes = head.shape[1]
    top = jnp.pad(norms, ((0, 0), (0, 64)))
    row = jnp.pad(bias[None, :], ((0, 1), (0, 128 - classes)))
    return jnp.concatenate([top, row, jnp.pad(head.T, ((0, 16 - classes), (0, 64)))], axis=0)


def pack_maps(features):
    images, height, width, channels = features.shape
    return jnp.reshape(jnp.transpose(features, (1, 0, 2, 3)), (height * images, width * channels))


def shards(train_features, train_labels, test_features, conv_first, conv_second, norm_params, head_weight, head_bias,
           mom_first, mom_second, mom_norm, mom_head, mom_bias, step_size):
    n = lax.axis_size("dp")
    chains = lax.axis_size("chain")
    me = lax.axis_index("dp")
    per = CH // n
    base = TAPS * per
    classes = head_weight.shape[2]
    images = train_features.shape[0]
    tests = test_features.shape[0]

    def pack(first, second):
        joined = jnp.concatenate([first, second], axis=2)
        return jnp.transpose(jnp.reshape(joined, (TAPS, n, per, 128)), (1, 0, 2, 3)).reshape(n, base, 128)

    theta = pack(conv_first[0], conv_second[0])
    mom_all = pack(mom_first[0], mom_second[0])
    mom = lax.dynamic_index_in_dim(mom_all, me, 0, keepdims=False)
    small = pack_small(norm_params[0], head_weight[0], head_bias[0])
    small_mom = pack_small(mom_norm[0], mom_head[0], mom_bias[0])
    train = pack_maps(train_features)
    test = pack_maps(test_features)
    hot = (train_labels[:, None] == jnp.arange(16, dtype=jnp.int32)[None, :]).astype(F32)

    def shape(*dims):
        return jax.ShapeDtypeStruct(dims, F32)

    def evaluate(theta, small):
        return pl.pallas_call(
            functools.partial(grad_kernel, classes),
            out_shape=shape(n, base + SMALL, 128),
            in_specs=[vmem()] * 4,
            out_specs=vmem(),
            scratch_shapes=compute_scratch(train.shape[0], train.shape[1], images, True),
            compiler_params=pltpu.CompilerParams(vmem_limit_bytes=50 << 20),
            name="gradient",
        )(train, hot, theta, small)

    pairs = [pltpu.SemaphoreType.DMA((n,))] * 2

    def move(index, factor, grads, theta, mom, small, small_mom):
        return pl.pallas_call(
            functools.partial(move_kernel, factor),
            out_shape=[shape(n, base, 128), shape(base, 128), shape(SMALL, 128), shape(SMALL, 128),
                       shape(base, 128), shape(SMALL, 128)],
            in_specs=[pl.BlockSpec(memory_space=pltpu.SMEM)] + [vmem()] * 5,
            out_specs=[vmem()] * 6,
            scratch_shapes=[pltpu.VMEM((n, base + SMALL, 128), F32), pltpu.VMEM((base, 128), F32)] + pairs + pairs,
            compiler_params=pltpu.CompilerParams(collective_id=index, has_side_effects=True),
            name="move%d" % index,
        )(step_size, grads, theta, mom, small, small_mom)

    start = 0.5 * (jnp.sum(theta * theta) + jnp.sum(small * small))
    start_kinetic = 0.5 * (jnp.sum(mom_all * mom_all) + jnp.sum(small_mom * small_mom))
    grads = evaluate(theta, small)
    theta, mom, small, small_mom, force_a, sums_a = move(0, 0.5, grads, theta, mom, small, small_mom)
    grads = evaluate(theta, small)
    theta, mom, small, small_mom, force_b, _ = move(1, 1.0, grads, theta, mom, small, small_mom)
    grads = evaluate(theta, small)
    probs = pl.pallas_call(
        functools.partial(test_kernel, classes),
        out_shape=shape(tests, 128),
        in_specs=[vmem()] * 3,
        out_specs=vmem(),
        scratch_shapes=compute_scratch(test.shape[0], test.shape[1], tests, False),
        compiler_params=pltpu.CompilerParams(vmem_limit_bytes=50 << 20),
        name="predict",
    )(test, theta, small)
    force, sums_b, kinetic, mean = pl.pallas_call(
        last_kernel,
        out_shape=[shape(base, 128), shape(SMALL, 128), shape(1, 128), shape(tests, 128)],
        in_specs=[pl.BlockSpec(memory_space=pltpu.SMEM)] + [vmem()] * 8,
        out_specs=[vmem()] * 4,
        scratch_shapes=[pltpu.VMEM((n, base + SMALL, 128), F32), pltpu.VMEM((8, 128), F32),
                        pltpu.VMEM((n, 8, 128), F32), pltpu.VMEM((chains, tests, 128), F32)]
        + pairs + pairs + [pltpu.SemaphoreType.DMA((chains,))] * 2,
        compiler_params=pltpu.CompilerParams(collective_id=2, has_side_effects=True),
        name="finish",
    )(step_size, grads, theta, mom, small, small_mom, force_a, force_b, probs)
    energy_start = sums_a[7, 0] + start
    energy_end = sums_b[7, 0] + 0.5 * (jnp.sum(theta * theta) + jnp.sum(small * small))
    potentials = jnp.stack([energy_start, energy_end])[None]
    pair = potentials + jnp.stack([start_kinetic, 0.5 * jnp.sum(kinetic)])[None]
    both = jnp.reshape(force, (TAPS, per, 2, 64))
    forces = jnp.transpose(both, (2, 0, 1, 3))[None]
    return mean[:, :classes], pair, potentials, forces


def solution(mesh):
    placed = (
        P("dp", None, None, None),
        P("dp"),
        P("dp", None, None, None),
        P("chain", None, None, None),
        P("chain", None, None, None),
        P("chain", None, None),
        P("chain", None, None),
        P("chain", None),
        P("chain", None, None, None),
        P("chain", None, None, None),
        P("chain", None, None),
        P("chain", None, None),
        P("chain", None),
        P("chain"),
    )
    return jax.shard_map(
        shards,
        mesh=mesh,
        in_specs=placed,
        out_specs=(
            P("dp", None),
            P("chain", None),
            P("chain", None),
            P("chain", None, None, "dp", None),
        ),
        check_vma=False,
    )
```

time: 638 us -> 132 us (0.21); the launches traced: 629 us -> 131 us
  matrix products: 275 us -> 0 us
  waiting for transfers between devices: 172 us -> 0 us
  blocking collectives: 116 us -> 0 us
  Pallas kernels: 0 us -> 92.7 us
  between operations: 30.8 us -> 7.44 us
  other arithmetic: 35 us -> 12.9 us
  local copies, waits for them, and re-layouts: 0.35 us -> 17.8 us
    dot_general x151 -> x0, matrix products: 256 us -> none  [the longest x141 253 us: conv_layer(): jnp.einsum('bhwc,cd->bhwd', window, kernel[offset], precision=highest)]
    psum x3 -> x0, waiting for transfers between devices: 172 us -> none  [reduce_all(): summed = lax.psum(others, 'dp')]
    psum x4 -> x0, blocking collectives: 116 us -> none  [the longest x2 74.3 us: reduce_all(): summed = lax.psum(others, 'dp')]
    pallas_call x0 -> x7, Pallas kernels: none -> 92.7 us  [the longest x2 46.5 us: move(): pl.pallas_call(functools.partial(move_kernel, factor), out_shape=[shape(n...]
    pad x12 -> x0, matrix products: 18.8 us -> none  [conv_layer(): window = padded[:, row_off:row_off + height, col_off:col_off + breadth, :]]
    reduce_sum x25 -> x6, other arithmetic: 21.4 us -> 9.78 us  [the longest x1 1.91 us: shards(): jnp.sum(mom_all * mom_all) + jnp.sum(small_mom * small_mom)]
    unnamed x144 -> x31, local copies, waits for them, and re-layouts: 0.33 us -> 10.8 us
    add_any x18 -> x0, other arithmetic: 7.1 us -> none  [the longest x6 4.41 us: conv_layer(): kernel[offset]]
  transfers between devices with their start and end apart: 3 -> 0, of which waited for: 3 -> 0; matrix products, arithmetic and copies ran while one was open for 1% -> 0% of each run, Pallas kernels for 0% -> 0%
where the time goes in v1:
time: 132 us; the launch traced here: 131 us
  Pallas kernels  92.7 us (70%)
  local copies, waits for them, and re-layouts  17.8 us (13%)
  other arithmetic  12.9 us (10%)
  between operations  7.44 us (6%)
    pallas_call x2, Pallas kernels, move(): pl.pallas_call(functools.partial(move_kernel, factor), out_shape=[shape(n...  46.5 us
    pallas_call x1, Pallas kernels, shards(): pl.pallas_call(last_kernel, out_shape=[shape(base, 128), shape(SMALL, 128...  21.4 us
    pallas_call x3, Pallas kernels, evaluate(): pl.pallas_call(functools.partial(grad_kernel, classes), out_shape=shape(n...  20 us
    unnamed x31, local copies, waits for them, and re-layouts  10.8 us
    pallas_call x1, Pallas kernels, shards(): pl.pallas_call(functools.partial(test_kernel, classes), out_shape=shape(t...  4.79 us

profile of v1, /device:TPU:0, one launch (start us, length us, event | category | flops | bytes accessed | tf_op | source)
XLA Modules:
  0.0 130.9 jit_solution(11672285947595663782)
XLA Ops:
  1.4 1.8 %fusion = f32[]{:T(128)} fusion(f32[9,8,8,64]{3,2,1,0:T(8,128)} %bitcast.58, f32[9,8,8,64]{3,2,1,0:T(8,128)} %bitcast.60), kind=kLoop, calls=%fused_computation.3 | loop fusion | flops 221183 | bytes 294916 | tf_op jit(solution)/shard_map/reduce_sum | solution.py:391
  3.2 0.7 copy.43
  3.9 0.7 copy.42
  4.6 0.7 copy.41
  5.2 0.7 copy.40
  5.9 1.9 %multiply_reduce_fusion.2 = (f32[]{:T(128)}, f32[24,128]{1,0:T(8,128)}, f32[]{:T(128)}, f32[24,128]{1,0:T(8,128)S(1)}) fusion(f32[10,64]{1,0:T(8,128)S(1)} %bitcast.69, f32[1,10]{1,0:T(1,128)} %param.26, f32[6,64]{1,0:T(8,128)S(1)} %bitcast.71, f32[10,64]{1,0:T(8,128)S(1)} %bitcast.68, f32[1,10]{1,0:T(1,128)} %param.21, f32[6,64]{1,0:T(8,128)S(1)} %bitcast.70), kind=kLoop, calls=%fused_computation.20 | loop fusion | flops 58366 | bytes 32856 | tf_op jit(solution)/shard_map/reduce_sum | solution.py:392
  9.1 0.7 fusion.1.hot_ref
  9.9 1.2 copy_bitcast_fusion.1.theta
  11.1 1.9 %multiply_reduce_fusion = (f32[]{:T(128)}, f32[8,9,8,128]{3,2,0,1:T(8,128)S(1)}) fusion(f32[9,8,8,64]{3,2,1,0:T(8,128)} %bitcast.64, f32[9,8,8,64]{3,2,1,0:T(8,128)} %bitcast.65), kind=kLoop, calls=%fused_computation.5 | loop fusion | flops 221183 | bytes 589828 | tf_op jit(solution)/shard_map/reduce_sum | solution.py:392
  15.3 6.6 %gradient.3.grads = f32[8,96,128]{2,1,0:T(8,128)S(1)} custom-call(f32[256,512]{1,0:T(8,128)S(1)} %reshape.94.x_ref, f32[32,16]{1,0:T(8,128)S(1)} %fusion.1.hot_ref, f32[8,72,128]{2,1,0:T(8,128)S(1)} %copy_bitcast_fusion.1.theta, f32[24,128]{1,0:T(8,128)S(1)} %get-tuple-element.45.small), custom_call_target="tpu_custom_call" | custom-call | tf_op jit(solution)/shard_map/gradient/pallas_call | solution.py:367
  21.9 0.7 copy-done.4
  22.7 24.1 %move0.1 = (f32[8,72,128]{2,1,0:T(8,128)}, f32[72,128]{1,0:T(8,128)}, f32[24,128]{1,0:T(8,128)}, f32[24,128]{1,0:T(8,128)}, f32[72,128]{1,0:T(8,128)}, /*index=5*/f32[24,128]{1,0:T(8,128)}) custom-call(f32[1]{0:T(128)S(6)} %copy.44.step, f32[8,96,128]{2,1,0:T(8,128)} %copy-done.4, f32[8,72,128]{2,1,0:T(8,128)} %copy-done.2, ...), custom_call_target="tpu_custom_call" | custom-call | tf_op jit(solution)/shard_map/move0/pallas_call | solution.py:380
  46.7 1.2 slice.10
  48.6 1.0 copy-done.6
  49.5 0.7 copy-done.11
  50.2 6.8 %gradient.4.grads = f32[8,96,128]{2,1,0:T(8,128)S(1)} custom-call(f32[256,512]{1,0:T(8,128)S(1)} %reshape.94.x_ref, f32[32,16]{1,0:T(8,128)S(1)} %fusion.1.hot_ref, f32[8,72,128]{2,1,0:T(8,128)S(1)} %copy-done.6, f32[24,128]{1,0:T(8,128)S(1)} %copy-done.11), custom_call_target="tpu_custom_call" | custom-call | tf_op jit(solution)/shard_map/gradient/pallas_call | solution.py:367
  57.1 0.7 copy-done.5
  57.8 22.4 %move1.1 = (f32[8,72,128]{2,1,0:T(8,128)}, f32[72,128]{1,0:T(8,128)}, f32[24,128]{1,0:T(8,128)}, f32[24,128]{1,0:T(8,128)}, f32[72,128]{1,0:T(8,128)}, /*index=5*/f32[24,128]{1,0:T(8,128)}) custom-call(f32[1]{0:T(128)S(6)} %copy.44.step, f32[8,96,128]{2,1,0:T(8,128)} %copy-done.5, f32[8,72,128]{2,1,0:T(8,128)} %get-tuple-element.19.theta, ...), custom_call_target="tpu_custom_call" | custom-call | tf_op jit(solution)/shard_map/move1/pallas_call | solution.py:380
  80.2 1.3 %multiply_reduce_fusion.3 = f32[]{:T(128)} fusion(f32[24,128]{1,0:T(8,128)} %get-tuple-element.24.small), kind=kLoop, calls=%fused_computation.21 | loop fusion | flops 6143 | bytes 12292 | tf_op jit(solution)/shard_map/reduce_sum | solution.py:419
  81.5 1.6 %multiply_reduce_fusion.1 = f32[]{:T(128)} fusion(f32[8,72,128]{2,1,0:T(8,128)} %get-tuple-element.23.theta), kind=kLoop, calls=%fused_computation.6 | loop fusion | flops 147455 | bytes 294916 | tf_op jit(solution)/shard_map/reduce_sum | solution.py:419
  84.5 1.0 copy-done
  85.4 0.7 copy-done.7
  86.1 6.6 %gradient.5.grads = f32[8,96,128]{2,1,0:T(8,128)S(1)} custom-call(f32[256,512]{1,0:T(8,128)S(1)} %reshape.94.x_ref, f32[32,16]{1,0:T(8,128)S(1)} %fusion.1.hot_ref, f32[8,72,128]{2,1,0:T(8,128)S(1)} %copy-done, f32[24,128]{1,0:T(8,128)S(1)} %copy-done.7), custom_call_target="tpu_custom_call" | custom-call | tf_op jit(solution)/shard_map/gradient/pallas_call | solution.py:367
  92.8 0.7 copy-done.3
  93.5 1.7 %copy.22 = f32[8,64,8,64]{3,2,1,0:T(8,128)S(1)} copy(f32[8,64,8,64]{3,2,0,1:T(8,128)} %bitcast.57) | data formatting | bytes 2097152 | tf_op jit(solution)/shard_map/transpose | solution.py:336
  96.2 4.8 %predict.1.probs = f32[64,128]{1,0:T(8,128)S(1)} custom-call(f32[512,512]{1,0:T(8,128)S(1)} %reshape.97.x_ref, f32[8,72,128]{2,1,0:T(8,128)S(1)} %copy-done.1, f32[24,128]{1,0:T(8,128)S(1)} %copy-done.8), custom_call_target="tpu_custom_call" | custom-call | tf_op jit(solution)/shard_map/predict/pallas_call | solution.py:398
  101.6 21.4 %finish.1 = (f32[72,128]{1,0:T(8,128)}, f32[24,128]{1,0:T(8,128)}, f32[1,128]{1,0:T(1,128)}, f32[64,128]{1,0:T(8,128)}) custom-call(f32[1]{0:T(128)S(6)} %copy.44.step, f32[8,96,128]{2,1,0:T(8,128)} %copy-done.3, f32[8,72,128]{2,1,0:T(8,128)} %get-tuple-element.23.theta, f32[72,128]{1,0:T(8,128)} %get-tuple-element.25.mom, ...), custom_call_target="tpu_custom_call" | custom-call | tf_op jit(solution)/shard_map/finish/pallas_call | solution.py:407
  123.0 1.2 reduce_sum.69
  124.9 1.2 slice.11
  127.3 1.4 %copy.24 = f32[64,10]{0,1:T(8,128)} copy(f32[64,10]{1,0:T(8,128)} %bitcast.67) | data formatting | bytes 5120
  129.4 0.9 reshape.98
  130.2 0.6 copy.39
  (26 shorter events, 3.7 us)
Async XLA Ops:
  0.6 14.3 %copy-start.12 = (f32[32,8,8,64]{3,2,1,0:T(8,128)S(1)}, f32[32,8,8,64]{3,2,1,0:T(8,128)}, u32[]{:S(2)}) copy-start(f32[32,8,8,64]{3,2,1,0:T(8,128)} %param.14) | copy-start | bytes 1572868
  7.8 7.5 %copy-start.10 = (f32[24,128]{1,0:T(8,128)}, f32[24,128]{1,0:T(8,128)S(1)}, u32[]{:S(2)}) copy-start(f32[24,128]{1,0:T(8,128)S(1)} %get-tuple-element.45.small) | copy-start | bytes 36868
  11.1 4.2 %copy-start.2 = (f32[8,72,128]{2,1,0:T(8,128)}, f32[8,72,128]{2,1,0:T(8,128)S(1)}, u32[]{:S(2)}) copy-start(f32[8,72,128]{2,1,0:T(8,128)S(1)} %copy_bitcast_fusion.1.theta) | copy-start | bytes 884740
  21.9 0.7 copy-start.4
  48.6 1.0 copy-start.6
  49.5 0.7 copy-start.11
  57.1 0.7 copy-start.5
  84.5 1.0 copy-start
  85.4 0.7 copy-start.7
  92.8 0.7 copy-start.3
  95.2 1.0 copy-start.1
  95.2 1.0 copy-start.8
  101.0 0.6 copy-start.9

commit v2 on v1

v2 whole, which is shorter than its diff:
```python
import functools

import jax
import jax.numpy as jnp
from jax import lax
from jax.experimental import pallas as pl
from jax.experimental.pallas import tpu as pltpu
from jax.sharding import PartitionSpec as P

MESH = pl.DeviceIdType.MESH
HIGHEST = lax.Precision.HIGHEST
EPS = 1e-6
CH = 64
TAPS = 9
SMALL = 16
F32 = jnp.float32
BF16 = jnp.bfloat16


def split(value):
    high = value.astype(BF16)
    return high, (value - high.astype(F32)).astype(BF16)


def mm(left, right):
    return jnp.dot(left, right, preferred_element_type=F32)


def put_weights(ref, taps):
    zero = jnp.zeros((CH, CH), F32)
    for a in range(3):
        mine = taps[3 * a : 3 * a + 3]
        left = jnp.concatenate(mine + [zero], axis=0)
        right = jnp.concatenate([zero] + mine, axis=0)
        high, low = split(jnp.concatenate([left, right], axis=1))
        ref[256 * a : 256 * a + 256, 0:128] = high
        ref[256 * a : 256 * a + 256, 128:256] = low


def put_padded(hs, ls, value, images):
    rows, width = value.shape
    edge = jnp.zeros((rows, CH), F32)
    high, low = split(jnp.concatenate([edge, value, edge], axis=1))
    block = jnp.zeros((images, width + 2 * CH), BF16)
    for ref, val in ((hs, high), (ls, low)):
        ref[0:images, :] = block
        ref[images : images + rows, :] = val
        ref[images + rows : 2 * images + rows, :] = block


def conv(hs, ls, weights, images):
    rows = hs.shape[0] - 2 * images
    outs = []
    for p in range((hs.shape[1] - 128) // 128):
        def window(ref):
            return jnp.concatenate(
                [ref[a * images : a * images + rows, 128 * p : 128 * p + 256] for a in range(3)], axis=1
            )
        both = mm(window(hs), weights[...])
        outs.append(both[:, :128] + both[:, 128:] + mm(window(ls), weights[:, :128]))
    return jnp.concatenate(outs, axis=1)


def kernel_grad(turned, hs, ls, images):
    high, low = turned
    width, rows = high.shape
    totals = [None] * 3
    for p in range(width // 128):
        part_high = high[128 * p : 128 * p + 128]
        stacked = jnp.concatenate([part_high, low[128 * p : 128 * p + 128]], axis=0)
        for a in range(3):
            start = (2 - a) * images
            both = mm(stacked, hs[start : start + rows, 128 * p : 128 * p + 256])
            both = both[:128] + both[128:]
            both = both + mm(part_high, ls[start : start + rows, 128 * p : 128 * p + 256])
            totals[a] = both if totals[a] is None else totals[a] + both
    grads = []
    for a in range(3):
        for b in range(3):
            grads.append(
                totals[a][0:64, (2 - b) * 64 : (3 - b) * 64] + totals[a][64:128, (3 - b) * 64 : (4 - b) * 64]
            )
    return grads


def over_columns(value):
    width = value.shape[1]
    shift = width // 2
    while shift >= CH:
        value = value + pltpu.roll(value, shift, 1)
        shift //= 2
    return value


def over_pixels(value, images):
    total = value[0:images]
    for h in range(1, value.shape[0] // images):
        total = total + value[h * images : (h + 1) * images]
    return over_columns(total)


def spread(value, rows):
    return jnp.concatenate([value] * (rows // value.shape[0]), axis=0)


def wide(row, width):
    return jnp.concatenate([row] * (width // CH), axis=1)


def above(value, bound):
    return jnp.where(value > bound, 1.0, jnp.where(value == bound, 0.5, 0.0))


def load_taps(theta, which):
    shards = theta.shape[0]
    per = CH // shards

    def tap(t):
        block = 8 if t == 8 else (t // 2 if which else 4 + t // 2)
        lane = 64 * (which if t == 8 else t % 2)
        return jnp.concatenate([theta[s, block * per : (block + 1) * per, lane : lane + 64] for s in range(shards)], axis=0)

    return [tap(t) for t in range(TAPS)]


def own_share(first, second, me, per):
    rows = pl.ds(pl.multiple_of(me * per, per), per)

    def pair(left, right):
        return jnp.concatenate([left, right], axis=1)

    blocks = [pair(second[0, 2 * i, rows, :], second[0, 2 * i + 1, rows, :]) for i in range(4)]
    blocks += [pair(first[0, 2 * i, rows, :], first[0, 2 * i + 1, rows, :]) for i in range(4)]
    return jnp.concatenate(blocks + [pair(first[0, 8, rows, :], second[0, 8, rows, :])], axis=0)


def head_rows(small):
    return jnp.concatenate([small[3:8, 0:64], small[3:8, 64:128], jnp.zeros((6, 64), F32)], axis=0)


def small_block(norms, head, bias, loss):
    return jnp.concatenate(
        [
            jnp.concatenate([norms[0:3], norms[3:6]], axis=1),
            jnp.concatenate([head[0:5], head[5:10]], axis=1),
            jnp.concatenate([bias, jnp.zeros((1, 48), F32), loss], axis=1),
            jnp.zeros((7, 128), F32),
        ],
        axis=0,
    )


def pack_small(norms, head, bias, square):
    classes = head.shape[2]
    square[...] = jnp.zeros_like(square)
    square[0:64, 0:classes] = head[0]
    turned = square[...].T
    square[0:1, :] = jnp.zeros((1, 128), F32)
    square[0:1, 0:classes] = bias[...]
    return small_block(norms[0], turned[0:16, 0:64], square[0:1, 0:16], jnp.zeros((1, 64), F32))


def forward(x, taps_one, taps_two, small, images, refs):
    hs, ls, ys, yl, w_one, w_two = refs
    rows, width = x.shape
    pixels = rows // images * (width // CH)
    put_weights(w_one, taps_one)
    put_weights(w_two, taps_two)
    norms = [wide(small[k % 3 : k % 3 + 1, 64 * (k // 3) : 64 * (k // 3) + 64], width) for k in range(6)]
    c1 = conv(hs, ls, w_one, images)
    r1 = spread(lax.rsqrt(over_pixels(c1 * c1, images) / pixels + EPS), rows)
    u1 = c1 * r1
    v1 = u1 * norms[0] + norms[1]
    y = jnp.maximum(v1, norms[2])
    put_padded(ys, yl, y, images)
    c2 = conv(ys, yl, w_two, images)
    r2 = spread(lax.rsqrt(over_pixels(c2 * c2, images) / pixels + EPS), rows)
    u2 = c2 * r2
    t = x + (u2 * norms[3] + norms[4])
    pooled = (over_pixels(jnp.maximum(t, norms[5]), images) / pixels)[:, 0:64]
    head = head_rows(small)
    logits = lax.dot_general(
        pooled, head, (((1,), (1,)), ((), ())), precision=HIGHEST, preferred_element_type=F32
    ) + small[8:9, 0:16]
    return norms, r1, u1, v1, y, r2, u2, t, pooled, head, logits


def soft(logits, classes):
    valid = lax.broadcasted_iota(jnp.int32, logits.shape, 1) < classes
    top = jnp.max(jnp.where(valid, logits, -jnp.inf), axis=1, keepdims=True)
    powers = jnp.where(valid, jnp.exp(jnp.where(valid, logits - top, 0.0)), 0.0)
    total = jnp.sum(powers, axis=1, keepdims=True)
    return powers / total, top + jnp.log(total)


def gradient(classes, x, hot, taps_one, taps_two, small, refs, early, late, send_early, send_late):
    xs, xl, ys, yl, gs, gl, w_one, w_two, w_back, turned_high, turned_low = refs
    rows, width = x.shape
    images = hot.shape[0]
    pixels = rows // images * (width // CH)
    norms, r1, u1, v1, y, r2, u2, t, pooled, head, logits = forward(
        x, taps_one, taps_two, small, images, (xs, xl, ys, yl, w_one, w_two)
    )
    probs, lse = soft(logits, classes)
    cross = jnp.sum(lse - jnp.sum(hot * logits, axis=1, keepdims=True), axis=0, keepdims=True)
    dlog = probs - hot
    dhead = lax.dot_general(dlog, pooled, (((0,), (0,)), ((), ())), precision=HIGHEST, preferred_element_type=F32)
    dbias = jnp.sum(dlog, axis=0, keepdims=True)
    dpool = jnp.dot(dlog, head, precision=HIGHEST, preferred_element_type=F32) / pixels
    dout = spread(wide(dpool, width), rows)
    dz = dout * above(t, norms[5])

    def by_channel(value):
        return over_columns(jnp.sum(value, axis=0, keepdims=True))[:, 0:64]

    dn5 = by_channel(dout - dz)
    dn4 = by_channel(dz)
    dn3 = by_channel(dz * u2)
    du = dz * norms[3]
    g2 = r2 * (du - u2 * spread(over_pixels(du * u2, images) / pixels, rows))
    put_padded(gs, gl, g2, images)
    grads_two = kernel_grad(split(y.T), gs, gl, images)
    shards = early.shape[0]
    per = CH // shards
    for i in range(4):
        both = jnp.concatenate([grads_two[2 * i], grads_two[2 * i + 1]], axis=1)
        for s in range(shards):
            early[s, i * per : (i + 1) * per, :] = both[s * per : (s + 1) * per]
    send_early()
    put_weights(w_back, [tap.T for tap in reversed(taps_two)])
    dy = conv(gs, gl, w_back, images)
    dv = dy * above(v1, norms[2])
    dn2 = by_channel(dy - dv)
    dn1 = by_channel(dv)
    dn0 = by_channel(dv * u1)
    du = dv * norms[0]
    g1 = r1 * (du - u1 * spread(over_pixels(du * u1, images) / pixels, rows))
    put_padded(ys, yl, g1, images)
    grads_one = kernel_grad((turned_high[...], turned_low[...]), ys, yl, images)
    block = small_block(
        jnp.concatenate([dn0, dn1, dn2, dn3, dn4, dn5], axis=0), dhead, dbias, jnp.broadcast_to(cross, (1, 64))
    )
    for i in range(5):
        both = jnp.concatenate([grads_one[2 * i], grads_two[8] if i == 4 else grads_one[2 * i + 1]], axis=1)
        for s in range(shards):
            late[s, i * per : (i + 1) * per, :] = both[s * per : (s + 1) * per]
    for s in range(shards):
        late[s, 5 * per : 5 * per + SMALL, :] = block
    send_late()


def greet(axes):
    barrier = pltpu.get_barrier_semaphore()
    count = 0
    for axis in axes:
        n = lax.axis_size(axis)
        me = lax.axis_index(axis)
        for k in range(1, n):
            pl.semaphore_signal(barrier, inc=1, device_id={axis: lax.rem(me + k, n)}, device_id_type=MESH)
        count += n - 1
    return lambda: pl.semaphore_wait(barrier, count)


def send_all(axis, source, slot, send_sem, recv_sem):
    n = lax.axis_size(axis)
    me = lax.axis_index(axis)
    copies = []
    for k in range(1, n):
        peer = lax.rem(me + k, n)
        copy = pltpu.make_async_remote_copy(
            src_ref=source(peer), dst_ref=slot(me), send_sem=send_sem.at[k], recv_sem=recv_sem.at[k],
            device_id={axis: peer}, device_id_type=MESH,
        )
        copy.start()
        copies.append(copy)
    return copies


def finish(copies):
    for copy in copies:
        copy.wait_recv()
    for copy in copies:
        copy.wait_send()


def in_order(ref):
    total = ref[0]
    for s in range(1, ref.shape[0]):
        total = total + ref[s]
    return total


def all_sum(value):
    while value.ndim > 2:
        value = jnp.sum(value, axis=0)
    return jnp.sum(jnp.sum(value, axis=0, keepdims=True), axis=1, keepdims=True)


def square_sum(value):
    return all_sum(value * value)


def whole_kernel(classes, step, x_ref, hot_ref, test_ref, first, second, norms, head, bias,
                 mom_first, mom_second, mom_norm, mom_head, mom_bias,
                 mean, hamiltonians, potentials, forces,
                 xs, xl, ys, yl, gs, gl, w_one, w_two, w_back, turned_high, turned_low, ts, tl, us, ul,
                 square, early, late, got_early, got_late, theta_all, small_all, share, small_mom, mom, mine, part,
                 parts, probs_own, seen, send_a, recv_a, send_b, recv_b, send_c, recv_c, send_d, recv_d, send_e, recv_e):
    n = lax.axis_size("dp")
    me = lax.axis_index("dp")
    chain = lax.axis_index("chain")
    per = CH // n
    h = step[0]
    arrived = greet(("dp", "chain"))
    x = x_ref[...]
    images = hot_ref.shape[0]
    tests = mean.shape[0]
    put_padded(xs, xl, x, images)
    turned_high[...], turned_low[...] = split(x.T)
    share[...] = own_share(first, second, me, per)
    mom[...] = own_share(mom_first, mom_second, me, per)
    small_all[0] = pack_small(norms, head, bias, square)
    small_mom[...] = pack_small(mom_norm, mom_head, mom_bias, square)
    refs = (xs, xl, ys, yl, gs, gl, w_one, w_two, w_back, turned_high, turned_low)
    line = lax.broadcasted_iota(jnp.int32, (SMALL, 128), 0)
    lane = lax.broadcasted_iota(jnp.int32, (SMALL, 128), 1)
    real = jnp.logical_or(line != 8, lane < 64)
    arrived()
    taps_one = [first[0, t] for t in range(TAPS)]
    taps_two = [second[0, t] for t in range(TAPS)]
    force = None
    for stage, factor in enumerate((0.5, 1.0, 0.5)):
        small = small_all.at[stage]
        copies = []

        def send_early():
            copies.extend(send_all("dp", lambda s: early.at[s], lambda s: got_early.at[stage, s],
                                   send_a.at[stage], recv_a.at[stage]))

        def send_late():
            copies.extend(send_all("dp", lambda s: late.at[s], lambda s: got_late.at[stage, s],
                                   send_b.at[stage], recv_b.at[stage]))

        gradient(classes, x, hot_ref[...], taps_one, taps_two, small, refs, early, late, send_early, send_late)
        got_early[stage, me] = early[me]
        got_late[stage, me] = late[me]
        if stage == 0:
            theta_squares = square_sum(first[0]) + square_sum(second[0]) + square_sum(small[...])
            mom_squares = square_sum(mom_first[0]) + square_sum(mom_second[0]) + square_sum(small_mom[...])
        if stage == 2:
            xt = test_ref[...]
            put_padded(ts, tl, xt, tests)
            logits = forward(xt, taps_one, taps_two, small, tests, (ts, tl, us, ul, w_one, w_two))[-1]
            probs_own[...] = jnp.concatenate([soft(logits, classes)[0], jnp.zeros((tests, 112), F32)], axis=1)
            others = send_all("chain", lambda s: probs_own, lambda s: seen.at[s], send_d, recv_d)
            seen[chain] = probs_own[...]
            share_squares = jnp.sum(share[...] * share[...], axis=0, keepdims=True)
        finish(copies)
        late_sum = in_order(got_late.at[stage])
        grad = jnp.concatenate([in_order(got_early.at[stage]), late_sum[0 : 5 * per]], axis=0) + share[...]
        sums = late_sum[5 * per : 5 * per + SMALL]
        mom_next = mom[...] - (factor * h) * grad
        small_grad = jnp.where(real, sums + small[...], 0.0)
        small_next = small_mom[...] - (factor * h) * small_grad
        weight = 0.5 if stage != 1 else 1.0
        force = weight * grad if force is None else force + weight * grad
        if stage < 2:
            mine[...] = share[...] + h * mom_next
            copies = send_all("dp", lambda s: mine, lambda s: theta_all.at[stage, s], send_c.at[stage], recv_c.at[stage])
            theta_all[stage, me] = mine[...]
            share[...] = mine[...]
            mom[...] = mom_next
            small_mom[...] = small_next
            small_all[stage + 1] = small[...] + h * small_next
            if stage == 0:
                energy_start = sums[8:9, 64:65] + 0.5 * theta_squares
            finish(copies)
            taps_one = load_taps(theta_all.at[stage], 0)
            taps_two = load_taps(theta_all.at[stage], 1)
    part[...] = jnp.concatenate(
        [jnp.sum(mom_next * mom_next, axis=0, keepdims=True), share_squares, jnp.zeros((6, 128), F32)], axis=0
    )
    copies = send_all("dp", lambda s: part, lambda s: parts.at[s], send_e, recv_e)
    parts[me] = part[...]
    for i in range(4):
        rows = slice(i * per, (i + 1) * per)
        for which, at in ((1, slice(i * per, (i + 1) * per)), (0, slice((4 + i) * per, (5 + i) * per))):
            forces[0, which, 2 * i] = force[at, 0:64]
            forces[0, which, 2 * i + 1] = force[at, 64:128]
    forces[0, 0, 8] = force[8 * per : 9 * per, 0:64]
    forces[0, 1, 8] = force[8 * per : 9 * per, 64:128]
    finish(others)
    mean[...] = (in_order(seen) / lax.axis_size("chain"))[:, 0:classes]
    small_squares = square_sum(small_all[2])
    kinetic_small = square_sum(small_next)
    finish(copies)
    both = in_order(parts)
    energy_end = sums[8:9, 64:65] + 0.5 * (all_sum(both[1:2]) + small_squares)
    pot = jnp.concatenate([energy_start, energy_end], axis=1)
    potentials[...] = pot
    hamiltonians[...] = pot + 0.5 * jnp.concatenate([mom_squares, all_sum(both[0:1]) + kinetic_small], axis=1)


def pack_maps(features):
    images, height, width, channels = features.shape
    return jnp.reshape(jnp.transpose(features, (1, 0, 2, 3)), (height * images, width * channels))


def vmem():
    return pl.BlockSpec(memory_space=pltpu.VMEM)


def shards(train_features, train_labels, test_features, *rest):
    n = lax.axis_size("dp")
    chains = lax.axis_size("chain")
    per = CH // n
    classes = rest[3].shape[2]
    images = train_features.shape[0]
    tests = test_features.shape[0]
    train = pack_maps(train_features)
    test = pack_maps(test_features)
    hot = (train_labels[:, None] == jnp.arange(16, dtype=jnp.int32)[None, :]).astype(F32)
    rows, width = train.shape
    small_maps = [pltpu.VMEM((rows + 2 * images, width + 128), BF16)] * 6
    large_maps = [pltpu.VMEM((test.shape[0] + 2 * tests, width + 128), BF16)] * 4

    def shape(*dims):
        return jax.ShapeDtypeStruct(dims, F32)

    def buffer(*dims):
        return pltpu.VMEM(dims, F32)

    def pair(*dims):
        return [pltpu.SemaphoreType.DMA(dims)] * 2

    return pl.pallas_call(
        functools.partial(whole_kernel, classes),
        out_shape=(shape(tests, classes), shape(1, 2), shape(1, 2), shape(1, 2, TAPS, per, 64)),
        in_specs=[pl.BlockSpec(memory_space=pltpu.SMEM)] + [vmem()] * 13,
        out_specs=[vmem()] * 4,
        scratch_shapes=small_maps + [pltpu.VMEM((768, 256), BF16)] * 3 + [pltpu.VMEM((width, rows), BF16)] * 2
        + large_maps
        + [buffer(128, 128), buffer(n, 4 * per, 128), buffer(n, 5 * per + SMALL, 128),
           buffer(3, n, 4 * per, 128), buffer(3, n, 5 * per + SMALL, 128), buffer(2, n, 9 * per, 128),
           buffer(3, SMALL, 128), buffer(9 * per, 128), buffer(SMALL, 128), buffer(9 * per, 128), buffer(9 * per, 128),
           buffer(8, 128), buffer(n, 8, 128), buffer(tests, 128), buffer(chains, tests, 128)]
        + pair(3, n) + pair(3, n) + pair(2, n) + pair(chains) + pair(n),
        compiler_params=pltpu.CompilerParams(
            collective_id=0, has_side_effects=True, vmem_limit_bytes=56 << 20
        ),
        name="leapfrog",
    )(rest[-1], train, hot, test, *rest[:-1])


def solution(mesh):
    placed = (
        P("dp", None, None, None),
        P("dp"),
        P("dp", None, None, None),
        P("chain", None, None, None),
        P("chain", None, None, None),
        P("chain", None, None),
        P("chain", None, None),
        P("chain", None),
        P("chain", None, None, None),
        P("chain", None, None, None),
        P("chain", None, None),
        P("chain", None, None),
        P("chain", None),
        P("chain"),
    )
    return jax.shard_map(
        shards,
        mesh=mesh,
        in_specs=placed,
        out_specs=(
            P("dp", None),
            P("chain", None),
            P("chain", None),
            P("chain", None, None, "dp", None),
        ),
        check_vma=False,
    )
```

time: 132 us -> 84.2 us (0.64)
  Pallas kernels: 92.7 us -> 69.6 us
  other arithmetic: 12.9 us -> 0.67 us
  between operations: 7.44 us -> 1.34 us
  local copies, waits for them, and re-layouts: 17.8 us -> 12.2 us
    pallas_call x7 -> x1, Pallas kernels: 92.7 us -> 69.6 us  [shards(): pl.pallas_call(functools.partial(whole_kernel, classes), out_shape=(shape...]
    reduce_sum x6 -> x0, other arithmetic: 9.78 us -> none  [the longest x1 1.91 us: shards(): jnp.sum(mom_all * mom_all) + jnp.sum(small_mom * small_mom)]
    unnamed x31 -> x19, local copies, waits for them, and re-layouts: 10.8 us -> 6.48 us
    slice x2 -> x0, local copies, waits for them, and re-layouts: 2.37 us -> none  [the longest x1 1.19 us: shards(): energy_start = sums_a[7, 0] + start]
    reshape x2, local copies, waits for them, and re-layouts: 0.76 us -> 2.53 us  [pack_maps(): jnp.reshape(jnp.transpose(features, (1, 0, 2, 3)), (height * images, widt...]
    reshape x2 -> x0, local copies, waits for them, and re-layouts: 1.5 us -> none  [shards(): both = jnp.reshape(force, (TAPS, per, 2, 64))]
    pallas_call x0 -> x1, local copies, waits for them, and re-layouts: none -> 1.43 us  [shards(): pl.pallas_call(functools.partial(whole_kernel, classes), out_shape=(shape...]
where the time goes in v2:
time: 84.2 us; the launch traced here: 83.8 us
  Pallas kernels  69.6 us (83%)
  local copies, waits for them, and re-layouts  12.2 us (14%)
  between operations  1.34 us (2%)
    pallas_call x1, Pallas kernels, shards(): pl.pallas_call(functools.partial(whole_kernel, classes), out_shape=(shape...  69.6 us
    unnamed x19, local copies, waits for them, and re-layouts  6.48 us
    reshape x2, local copies, waits for them, and re-layouts, pack_maps(): jnp.reshape(jnp.transpose(features, (1, 0, 2, 3)), (height * images, widt...  2.53 us
    transpose x2, local copies, waits for them, and re-layouts, pack_maps(): jnp.transpose(features, (1, 0, 2, 3))  1.8 us

profile of v2, /device:TPU:0, one launch (start us, length us, event | category | flops | bytes accessed | tf_op | source)
XLA Modules:
  0.0 83.8 jit_solution(9619316962211542633)
XLA Ops:
  0.6 1.7 %copy.19 = f32[8,64,8,64]{3,2,1,0:T(8,128)S(1)} copy(f32[8,64,8,64]{3,2,0,1:T(8,128)} %bitcast.6) | data formatting | bytes 2097152 | tf_op jit(solution)/shard_map/transpose | solution.py:406
  2.4 0.0 copy-start
  2.4 1.5 %reshape.16.test_ref = f32[512,512]{1,0:T(8,128)} reshape(f32[8,64,8,64]{3,2,1,0:T(8,128)S(1)} %copy.19) | data formatting | bytes 2097152 | tf_op jit(solution)/shard_map/reshape | solution.py:406
  3.8 0.0 copy-start.1
  3.8 0.0 copy-start.2
  3.8 0.0 copy-start.5
  3.8 0.0 copy-start.3
  3.8 0.0 copy-start.4
  3.9 0.0 copy-done
  3.9 0.1 copy.18
  3.9 1.1 %reshape.15.x_ref = f32[256,512]{1,0:T(8,128)} reshape(f32[8,32,8,64]{3,2,1,0:T(8,128)S(1)} %copy.18) | data formatting | bytes 1048576 | tf_op jit(solution)/shard_map/reshape | solution.py:406
  5.0 0.0 copy-done.1
  5.0 0.7 copy.21.head
  5.7 0.0 copy-done.2
  5.7 0.7 copy.23.mom_head
  6.4 0.0 copy-done.5
  6.4 0.7 fusion.hot_ref
  7.1 0.0 copy-done.3
  7.1 0.6 copy.20.norms
  7.7 0.0 copy-done.4
  7.7 0.6 copy.22.mom_norm
  8.9 69.6 %leapfrog.1 = (f32[64,10]{1,0:T(8,128)}, f32[1,2]{1,0:T(1,128)}, f32[1,2]{1,0:T(1,128)}, f32[1,2,9,8,64]{4,3,2,1,0:T(8,128)}) custom-call(f32[1]{0:T(128)S(6)} %copy.28.step, f32[256,512]{1,0:T(8,128)} %reshape.15.x_ref, f32[32,16]{1,0:T(8,128)} %fusion.hot_ref, f32[512,512]{1,0:T(8,128)} %reshape.16.test_ref, f32[1,9,64,64]{3,2,1,0:T(8,128)} %first.1, ...), custom_call_target="tpu_custom_call" | custom-call | tf_op jit(solution)/shard_map/leapfrog/pallas_call | solution.py:436
  78.5 1.4 %copy.24 = f32[64,10]{0,1:T(8,128)} copy(f32[64,10]{1,0:T(8,128)} %get-tuple-element.4) | data formatting | bytes 5120 | tf_op jit(solution)/shard_map/leapfrog/pallas_call | solution.py:436
  80.0 1.2 %copy.29 = f32[1,2]{1,0:T(1,128)} copy(f32[1,2]{1,0:T(1,128)} %get-tuple-element.13) | data formatting | bytes 16
  81.1 1.2 %copy.30 = f32[1,2]{1,0:T(1,128)} copy(f32[1,2]{1,0:T(1,128)} %get-tuple-element.14) | data formatting | bytes 16
  82.3 1.5 %copy.31 = f32[1,2,9,8,64]{4,3,2,1,0:T(8,128)} copy(f32[1,2,9,8,64]{4,3,2,1,0:T(8,128)} %get-tuple-element.15) | data formatting | bytes 73728
Async XLA Ops:
  2.4 1.5 %copy-start = (f32[32,8,8,64]{3,2,1,0:T(8,128)S(1)}, f32[32,8,8,64]{3,2,1,0:T(8,128)}, u32[]{:S(2)}) copy-start(f32[32,8,8,64]{3,2,1,0:T(8,128)} %param.14) | copy-start | bytes 1572868
  3.8 1.2 %copy-start.1 = (f32[1,64,10]{1,0,2:T(1,128)S(1)}, f32[1,64,10]{1,0,2:T(1,128)}, u32[]{:S(2)}) copy-start(f32[1,64,10]{1,0,2:T(1,128)} %param.20) | copy-start | bytes 7684
  3.8 1.9 %copy-start.2 = (f32[1,64,10]{1,0,2:T(1,128)S(1)}, f32[1,64,10]{1,0,2:T(1,128)}, u32[]{:S(2)}) copy-start(f32[1,64,10]{1,0,2:T(1,128)} %param.25) | copy-start | bytes 7684
  3.8 2.6 %copy-start.5 = (s32[32]{0:T(128)S(1)}, s32[32]{0:T(128)}, u32[]{:S(2)}) copy-start(s32[32]{0:T(128)} %param.15) | copy-start | bytes 388
  3.8 3.3 %copy-start.3 = (f32[1,6,64]{2,0,1:T(1,128)S(1)}, f32[1,6,64]{2,0,1:T(1,128)}, u32[]{:S(2)}) copy-start(f32[1,6,64]{2,0,1:T(1,128)} %param.19) | copy-start | bytes 4612
  3.8 3.8 %copy-start.4 = (f32[1,6,64]{2,0,1:T(1,128)S(1)}, f32[1,6,64]{2,0,1:T(1,128)}, u32[]{:S(2)}) copy-start(f32[1,6,64]{2,0,1:T(1,128)} %param.24) | copy-start | bytes 4612

commit v3 on v2

--- a/solution.py
+++ b/solution.py
@@ -150,14 +150,15 @@
     )
 
 
-def pack_small(norms, head, bias, square):
-    classes = head.shape[2]
-    square[...] = jnp.zeros_like(square)
-    square[0:64, 0:classes] = head[0]
-    turned = square[...].T
-    square[0:1, :] = jnp.zeros((1, 128), F32)
-    square[0:1, 0:classes] = bias[...]
-    return small_block(norms[0], turned[0:16, 0:64], square[0:1, 0:16], jnp.zeros((1, 64), F32))
+def pack_small(norms, head, bias, row):
+    classes = head.shape[0]
+    zero = jnp.zeros((1, 64), F32)
+    row[...] = jnp.zeros_like(row)
+    row[0:1, 0:classes] = bias[...]
+    lines = [head[k] for k in range(classes)] + [zero] * (16 - classes)
+    return small_block(
+        jnp.concatenate([norms[k] for k in range(6)], axis=0), jnp.concatenate(lines, axis=0), row[0:1, 0:16], zero
+    )
 
 
 def forward(x, taps_one, taps_two, small, images, refs):
@@ -265,7 +266,7 @@
     n = lax.axis_size(axis)
     me = lax.axis_index(axis)
     copies = []
-    for k in range(1, n):
+    for k in sorted(range(1, n), key=lambda k: -min(k, n - k)):
         peer = lax.rem(me + k, n)
         copy = pltpu.make_async_remote_copy(
             src_ref=source(peer), dst_ref=slot(me), send_sem=send_sem.at[k], recv_sem=recv_sem.at[k],
@@ -300,7 +301,7 @@
     return all_sum(value * value)
 
 
-def whole_kernel(classes, step, x_ref, hot_ref, test_ref, first, second, norms, head, bias,
+def whole_kernel(classes, step, x_ref, label_ref, test_ref, first, second, norms, head, bias,
                  mom_first, mom_second, mom_norm, mom_head, mom_bias,
                  mean, hamiltonians, potentials, forces,
                  xs, xl, ys, yl, gs, gl, w_one, w_two, w_back, turned_high, turned_low, ts, tl, us, ul,
@@ -313,7 +314,9 @@
     h = step[0]
     arrived = greet(("dp", "chain"))
     x = x_ref[...]
-    images = hot_ref.shape[0]
+    images = label_ref.shape[1]
+    spots = jnp.broadcast_to(label_ref[...], (128, images)) == lax.broadcasted_iota(jnp.int32, (128, images), 0)
+    hot = jnp.where(spots, 1.0, 0.0).T[:, 0:16]
     tests = mean.shape[0]
     put_padded(xs, xl, x, images)
     turned_high[...], turned_low[...] = split(x.T)
@@ -341,7 +344,7 @@
             copies.extend(send_all("dp", lambda s: late.at[s], lambda s: got_late.at[stage, s],
                                    send_b.at[stage], recv_b.at[stage]))
 
-        gradient(classes, x, hot_ref[...], taps_one, taps_two, small, refs, early, late, send_early, send_late)
+        gradient(classes, x, hot, taps_one, taps_two, small, refs, early, late, send_early, send_late)
         got_early[stage, me] = early[me]
         got_late[stage, me] = late[me]
         if stage == 0:
@@ -390,7 +393,7 @@
     forces[0, 0, 8] = force[8 * per : 9 * per, 0:64]
     forces[0, 1, 8] = force[8 * per : 9 * per, 64:128]
     finish(others)
-    mean[...] = (in_order(seen) / lax.axis_size("chain"))[:, 0:classes]
+    mean[...] = in_order(seen) / lax.axis_size("chain")
     small_squares = square_sum(small_all[2])
     kinetic_small = square_sum(small_next)
     finish(copies)
@@ -399,6 +402,13 @@
     pot = jnp.concatenate([energy_start, energy_end], axis=1)
     potentials[...] = pot
     hamiltonians[...] = pot + 0.5 * jnp.concatenate([mom_squares, all_sum(both[0:1]) + kinetic_small], axis=1)
+
+
+def deliver_kernel(mean, hamiltonians, potentials, forces, mean_out, hamiltonians_out, potentials_out, forces_out):
+    mean_out[...] = mean[...].T[0 : mean_out.shape[0]]
+    hamiltonians_out[...] = hamiltonians[...]
+    potentials_out[...] = potentials[...]
+    forces_out[...] = forces[...]
 
 
 def pack_maps(features):
@@ -419,7 +429,13 @@
     tests = test_features.shape[0]
     train = pack_maps(train_features)
     test = pack_maps(test_features)
-    hot = (train_labels[:, None] == jnp.arange(16, dtype=jnp.int32)[None, :]).astype(F32)
+    first, second, norms, head, bias, mom_first, mom_second, mom_norm, mom_head, mom_bias, step_size = rest
+
+    def lead(array, order):
+        return jnp.transpose(array, order)
+
+    rest = (first, second, lead(norms, (1, 0, 2)), lead(head, (2, 0, 1)), bias,
+            mom_first, mom_second, lead(mom_norm, (1, 0, 2)), lead(mom_head, (2, 0, 1)), mom_bias)
     rows, width = train.shape
     small_maps = [pltpu.VMEM((rows + 2 * images, width + 128), BF16)] * 6
     large_maps = [pltpu.VMEM((test.shape[0] + 2 * tests, width + 128), BF16)] * 4
@@ -433,14 +449,14 @@
     def pair(*dims):
         return [pltpu.SemaphoreType.DMA(dims)] * 2
 
-    return pl.pallas_call(
+    results = pl.pallas_call(
         functools.partial(whole_kernel, classes),
-        out_shape=(shape(tests, classes), shape(1, 2), shape(1, 2), shape(1, 2, TAPS, per, 64)),
+        out_shape=(shape(tests, 128), shape(1, 2), shape(1, 2), shape(1, 2, TAPS, per, 64)),
         in_specs=[pl.BlockSpec(memory_space=pltpu.SMEM)] + [vmem()] * 13,
         out_specs=[vmem()] * 4,
         scratch_shapes=small_maps + [pltpu.VMEM((768, 256), BF16)] * 3 + [pltpu.VMEM((width, rows), BF16)] * 2
         + large_maps
-        + [buffer(128, 128), buffer(n, 4 * per, 128), buffer(n, 5 * per + SMALL, 128),
+        + [buffer(8, 128), buffer(n, 4 * per, 128), buffer(n, 5 * per + SMALL, 128),
            buffer(3, n, 4 * per, 128), buffer(3, n, 5 * per + SMALL, 128), buffer(2, n, 9 * per, 128),
            buffer(3, SMALL, 128), buffer(9 * per, 128), buffer(SMALL, 128), buffer(9 * per, 128), buffer(9 * per, 128),
            buffer(8, 128), buffer(n, 8, 128), buffer(tests, 128), buffer(chains, tests, 128)]
@@ -449,7 +465,15 @@
             collective_id=0, has_side_effects=True, vmem_limit_bytes=56 << 20
         ),
         name="leapfrog",
-    )(rest[-1], train, hot, test, *rest[:-1])
+    )(step_size, train, jnp.reshape(train_labels, (1, images)), test, *rest)
+    mean, hamiltonians, potentials, forces = pl.pallas_call(
+        deliver_kernel,
+        out_shape=(shape(classes, tests), shape(1, 2), shape(1, 2), shape(1, 2, TAPS, per, 64)),
+        in_specs=[vmem()] * 4,
+        out_specs=[vmem()] * 4,
+        name="deliver",
+    )(*results)
+    return mean.T, hamiltonians, potentials, forces
 
 
 def solution(mesh):

time: 84.2 us -> 77.4 us (0.919)
  local copies, waits for them, and re-layouts: 12.2 us -> 4.33 us
  Pallas kernels: 69.6 us -> 71.3 us
    unnamed x19 -> x2, local copies, waits for them, and re-layouts: 6.48 us -> 0.01 us
    pallas_call x0 -> x1, Pallas kernels: none -> 1.59 us  [shards(): pl.pallas_call(deliver_kernel, out_shape=(shape(classes, tests), shape(1,...]
    pallas_call x1 -> x0, local copies, waits for them, and re-layouts: 1.43 us -> none  [shards(): pl.pallas_call(functools.partial(whole_kernel, classes), out_shape=(shape...]
where the time goes in v3:
time: 77.4 us; the launch traced here: 76.9 us
  Pallas kernels  71.3 us (92%)
  local copies, waits for them, and re-layouts  4.33 us (6%)
  between operations  1.31 us (2%)
    pallas_call x1, Pallas kernels, shards(): pl.pallas_call(functools.partial(whole_kernel, classes), out_shape=(shape...  69.7 us
    reshape x2, local copies, waits for them, and re-layouts, pack_maps(): jnp.reshape(jnp.transpose(features, (1, 0, 2, 3)), (height * images, widt...  2.53 us
    transpose x2, local copies, waits for them, and re-layouts, pack_maps(): jnp.transpose(features, (1, 0, 2, 3))  1.8 us
    pallas_call x1, Pallas kernels, shards(): pl.pallas_call(deliver_kernel, out_shape=(shape(classes, tests), shape(1,...  1.59 us

profile of v3, /device:TPU:0, one launch (start us, length us, event | category | flops | bytes accessed | tf_op | source)
XLA Modules:
  0.0 76.9 jit_solution(10583120027715581012)
XLA Ops:
  0.6 1.7 %copy.19 = f32[8,64,8,64]{3,2,1,0:T(8,128)S(1)} copy(f32[8,64,8,64]{3,2,0,1:T(8,128)} %bitcast.12) | data formatting | bytes 2097152 | tf_op jit(solution)/shard_map/transpose | solution.py:416
  2.4 0.0 copy-start
  2.4 1.5 %reshape.19.test_ref = f32[512,512]{1,0:T(8,128)} reshape(f32[8,64,8,64]{3,2,1,0:T(8,128)S(1)} %copy.19) | data formatting | bytes 2097152 | tf_op jit(solution)/shard_map/reshape | solution.py:416
  3.8 0.0 copy-done
  3.8 0.1 copy.18
  3.9 1.1 %reshape.17.x_ref = f32[256,512]{1,0:T(8,128)} reshape(f32[8,32,8,64]{3,2,1,0:T(8,128)S(1)} %copy.18) | data formatting | bytes 1048576 | tf_op jit(solution)/shard_map/reshape | solution.py:416
  5.6 69.7 %leapfrog.1 = (f32[64,128]{1,0:T(8,128)}, f32[1,2]{1,0:T(1,128)}, f32[1,2]{1,0:T(1,128)}, f32[1,2,9,8,64]{4,3,2,1,0:T(8,128)}) custom-call(f32[1]{0:T(128)S(6)} %copy.20.step, f32[256,512]{1,0:T(8,128)} %reshape.17.x_ref, s32[1,32]{1,0:T(1,128)} %bitcast.18, f32[512,512]{1,0:T(8,128)} %reshape.19.test_ref, f32[1,9,64,64]{3,2,1,0:T(8,128)} %first.1, ...), custom_call_target="tpu_custom_call" | custom-call | tf_op jit(solution)/shard_map/leapfrog/pallas_call | solution.py:452
  75.3 1.6 %deliver.1 = (f32[10,64]{1,0:T(8,128)}, f32[1,2]{1,0:T(1,128)}, f32[1,2]{1,0:T(1,128)}, f32[1,2,9,8,64]{4,3,2,1,0:T(8,128)}) custom-call(f32[64,128]{1,0:T(8,128)} %get-tuple-element.12.mean, f32[1,2]{1,0:T(1,128)} %get-tuple-element.13.hamiltonians, f32[1,2]{1,0:T(1,128)} %get-tuple-element.14.potentials, f32[1,2,9,8,64]{4,3,2,1,0:T(8,128)} %get-tuple-element.15.forces), custom_call_target="tpu_custom_call" | custom-call | tf_op jit(solution)/shard_map/deliver/pallas_call | solution.py:469
Async XLA Ops:
  2.4 1.5 %copy-start = (f32[32,8,8,64]{3,2,1,0:T(8,128)S(1)}, f32[32,8,8,64]{3,2,1,0:T(8,128)}, u32[]{:S(2)}) copy-start(f32[32,8,8,64]{3,2,1,0:T(8,128)} %param.14) | copy-start | bytes 1572868
